TPU v7x, 32 devices: a whole 2x2x4 slice. The times are simulated.
32 devices in a mesh: groups: 1, ep: 32 (over z, y, x, core).
Axes of the slice: x: 2, y: 2, z: 4, core: 2. Of those that a mesh axis runs over, the one named last changes fastest.
Arguments:
- queries: bfloat16 [128, 8, 16, 576], P(('groups', 'ep')), may hold values from -48 to 48
- cache: bfloat16 [128, 384, 576], P(('groups', 'ep')), may hold values from -4 to 4
- drafts: bfloat16 [128, 8, 576], P(('groups', 'ep')), may hold values from -8 to 8
- lengths: int32 [128], P(('groups', 'ep')), may hold values from 96 to 384
- value_up: bfloat16 [16, 512, 128], replicated, may hold values from -0.25 to 0.25
- residual: bfloat16 [1024, 2048], P(('groups', 'ep')), may hold values from -20 to 20
- norm_gain: float32 [2048], replicated, may hold values from 0.5 to 1.5
- w_gate: bfloat16 [32, 2048, 704], P('ep'), may hold values from -0.125 to 0.125
- w_up: bfloat16 [32, 2048, 704], P('ep'), may hold values from -0.125 to 0.125
- w_down: bfloat16 [32, 704, 2048], P('ep'), may hold values from -0.15625 to 0.15625
- routes: int32 [1024, 6], P(('groups', 'ep')), may hold values from 0 to 15, all different within a row; in each aligned block of 32 rows (0 to 31, 32 to 63, ...) at most 14 rows name the same one
- combine_weights: float32 [1024, 6], P(('groups', 'ep')), may hold values from 0.05 to 0.4
Outputs:
- layer_out: bfloat16 [1024, 2048], P(('groups', 'ep'))
Inputs may be any that keep to these rules, and one draw needn't show every extreme that they name: `routes`: among the rows of one device, no expert is named more than 14 times over all slots.
All inputs are finite; a program needn't handle non-finite values.
Results may differ from a plain program's by a relative error of at most 0.0043.
Values may be sent and summed in bfloat16 or wider, within the bound.
A program may use at most 64 MiB of HBM per device.

v0:
```python
import functools

import jax
import jax.numpy as jnp
from jax import lax
from jax.experimental import pallas as pl
from jax.experimental.pallas import tpu as pltpu
from jax.sharding import PartitionSpec as P


BF = jnp.bfloat16
F32 = jnp.float32


def up_to(value, unit):
    return -(-value // unit) * unit


def dot_rows(a, b):
    return lax.dot_general(a, b, (((1,), (1,)), ((), ())), preferred_element_type=F32)


def attend(query, cache, draft, length, heads, latent, scale):
    cached = jnp.dot(query, cache, preferred_element_type=F32) * scale
    own = dot_rows(query, draft) * scale
    visible = lax.broadcasted_iota(jnp.int32, cached.shape, 1) < length
    row = lax.broadcasted_iota(jnp.int32, own.shape, 0)
    causal = lax.broadcasted_iota(jnp.int32, own.shape, 1) * heads <= row
    cached = jnp.where(visible, cached, -1e30)
    own = jnp.where(causal, own, -1e30)
    highest = jnp.maximum(
        jnp.max(cached, axis=-1, keepdims=True), jnp.max(own, axis=-1, keepdims=True)
    )
    cached = jnp.exp(cached - highest)
    own = jnp.exp(own - highest)
    total = jnp.sum(cached, axis=-1, keepdims=True) + jnp.sum(own, axis=-1, keepdims=True)
    part = 1.0 / total
    mixed = dot_rows((cached * part).astype(BF), cache[:latent])
    mixed += jnp.dot((own * part).astype(BF), draft[:, :latent], preferred_element_type=F32)
    return mixed.astype(BF).astype(F32)


def tables(routes, weights, meta, slots):
    top, tokens = routes.shape
    planes, qs, lanes = meta.shape
    side = qs // slots
    experts = planes * side
    number = lax.broadcasted_iota(jnp.int32, (experts, tokens), 0)
    member = jnp.zeros((experts, tokens), F32)
    weight = jnp.zeros((experts, tokens), F32)
    for k in range(top):
        named = routes[k : k + 1, :] == number
        member = jnp.where(named, 1.0, member)
        weight = jnp.where(named, weights[k : k + 1, :], weight)
    before = lax.broadcasted_iota(jnp.int32, (tokens, tokens), 0)
    after = lax.broadcasted_iota(jnp.int32, (tokens, tokens), 1)
    earlier = jnp.where(before < after, 1.0, 0.0).astype(BF)
    slot = jnp.dot(member.astype(BF), earlier, preferred_element_type=F32)
    slot = jnp.where(member > 0.5, slot, -1.0)
    high = weight.astype(BF).astype(F32)
    rest = jnp.zeros((experts, lanes - 3 * tokens), F32)
    slot = jnp.concatenate([slot, slot, slot, rest - 1.0], axis=1)
    value = jnp.concatenate([member, high, weight - high, rest], axis=1)
    place = lax.broadcasted_iota(jnp.int32, (slots, lanes), 0).astype(F32)
    for e in range(experts):
        block = jnp.where(slot[e : e + 1] == place, value[e : e + 1], 0.0)
        at = e % side * slots
        meta[e // side, at : at + slots] = block.astype(BF)


def expert_kernel(
    planes,
    side,
    slots,
    lengths,
    routes,
    weights,
    drafts,
    residual,
    gain,
    q_hbm,
    cache_hbm,
    vup_hbm,
    gate_hbm,
    up_hbm,
    down_hbm,
    out,
    q_v,
    cache_v,
    vup,
    mixes,
    stream,
    normed,
    meta,
    w_gate,
    w_up,
    w_down,
    z_rows,
    z_meta,
    stage,
    rows,
    mine,
    pair_out,
    pair_in,
    back_out,
    back_in,
    part_out,
    part_in,
    total,
    q_sem,
    c_sem,
    v_sem,
    w_sem,
    zr_s,
    zr_r,
    zm_s,
    zm_r,
    ip_s,
    ip_r,
    fw_s,
    fw_r,
    pp_s,
    pp_r,
    rt_s,
    rt_r,
    fn_s,
    fn_r,
):
    tokens, width = normed.shape
    qs = side * slots
    me = lax.axis_index("ep")
    core = lax.rem(me, 2)
    other = 1 - core
    chip = me // 2
    z = chip // side
    q = lax.rem(chip, side)

    def at(zz, qq, cc):
        return {"ep": (zz * side + qq) * 2 + cc}

    def ahead(value, step, size):
        return lax.rem(value + step, size)

    def remote(src, dst, send, recv, device):
        return pltpu.make_async_remote_copy(
            src_ref=src,
            dst_ref=dst,
            send_sem=send,
            recv_sem=recv,
            device_id=device,
            device_id_type=pl.DeviceIdType.MESH,
        )

    reqs, draft_heads, _ = q_v.shape
    fetched = []
    for r in range(reqs):
        pair = [
            pltpu.make_async_copy(q_hbm.at[r], q_v.at[r], q_sem.at[r]),
            pltpu.make_async_copy(cache_hbm.at[r], cache_v.at[r], c_sem.at[r]),
        ]
        for load in pair:
            load.start()
        fetched.append(pair)
    vup_load = pltpu.make_async_copy(vup_hbm, vup, v_sem.at[0])
    vup_load.start()
    loads = [
        pltpu.make_async_copy(gate_hbm.at[0], w_gate, w_sem.at[0]),
        pltpu.make_async_copy(up_hbm.at[0], w_up, w_sem.at[1]),
        pltpu.make_async_copy(down_hbm.at[0], w_down, w_sem.at[2]),
    ]
    for load in loads:
        load.start()

    peers = [at(ahead(z, d, planes), q, core) for d in range(1, planes)]
    peers += [at(z, ahead(q, d, side), core) for d in range(1, side)]
    peers += [at(z, q, other)]
    barrier = pltpu.get_barrier_semaphore()
    for peer in peers:
        pl.semaphore_signal(
            barrier, inc=1, device_id=peer, device_id_type=pl.DeviceIdType.MESH
        )

    tables(routes, weights, meta, slots)
    heads, latent, head = vup.shape
    scale = (head + q_v.shape[2] - latent) ** (-0.5)
    for r in range(reqs):
        for load in fetched[r]:
            load.wait()
        mixed = attend(q_v[r], cache_v[r], drafts[r], lengths[r], heads, latent, scale)
        for g in range(latent // 128):
            mixes[g, r * draft_heads : (r + 1) * draft_heads] = mixed[
                :, g * 128 : (g + 1) * 128
            ]
    vup_load.wait()
    for h in range(heads):
        value = jnp.concatenate(
            [mixes[g, pl.ds(h, tokens, stride=heads), :] for g in range(latent // 128)], axis=1
        ).astype(BF)
        part = slice(h * head, (h + 1) * head)
        stream[:, part] = residual[:, part].astype(F32) + jnp.dot(
            value, vup[h], preferred_element_type=F32
        )
    value = stream[...]
    level = lax.rsqrt(jnp.mean(value * value, axis=-1, keepdims=True) + 1e-06)
    normed[...] = (value * level * gain[...]).astype(BF)
    pl.semaphore_wait(barrier, len(peers))

    sends = []

    def go(copy):
        copy.start()
        sends.append(copy)

    for d in range(1, planes):
        zd = ahead(z, d, planes)
        device = at(zd, q, core)
        go(remote(meta.at[zd], z_meta.at[d], zm_s.at[d], zm_r.at[d], device))
        go(remote(normed, z_rows.at[d], zr_s.at[d], zr_r.at[d], device))

    def behind(d):
        return ahead(z, planes - d, planes)

    def pick(d):
        if d:
            device = at(behind(d), q, core)
            remote(z_meta.at[d], z_meta.at[d], zm_s.at[d], zm_r.at[d], device).wait_recv()
            remote(normed, z_rows.at[d], zr_s.at[d], zr_r.at[d], device).wait_recv()
            table, values = z_meta[d], z_rows[d]
        else:
            table, values = meta[z], normed[...]
        picked = jnp.dot(table[:, :tokens], values, preferred_element_type=F32).astype(BF)
        stage[d] = picked.reshape(side, slots, width)
        rows[core, d, q] = stage[d, q]
        for k in range(1, side):
            qk = ahead(q, k, side)
            go(
                remote(
                    stage.at[d, qk],
                    rows.at[core, d, q],
                    ip_s.at[d, k],
                    ip_r.at[d, k],
                    at(z, qk, core),
                )
            )

    def forward(d):
        for k in range(1, side):
            qk = ahead(q, side - k, side)
            landing = rows.at[core, d, qk]
            remote(
                landing, landing, ip_s.at[d, k], ip_r.at[d, k], at(z, qk, core)
            ).wait_recv()
        go(
            remote(
                rows.at[core, d], rows.at[core, d], fw_s.at[d], fw_r.at[d], at(z, q, other)
            )
        )

    def compute(d):
        landing = rows.at[other, d]
        remote(landing, landing, fw_s.at[d], fw_r.at[d], at(z, q, other)).wait_recv()
        if d == 0:
            for load in loads:
                load.wait()
        x = jnp.concatenate(
            [rows[other, d].reshape(qs, width), rows[core, d].reshape(qs, width)], axis=0
        )
        gate = dot_rows(x, w_gate[...])
        upper = dot_rows(x, w_up[...])
        active = (gate / (1.0 + jnp.exp(-gate)) * upper).astype(BF)
        down = w_down[...]
        pair_out[d] = jnp.dot(active[:qs], down, preferred_element_type=F32).astype(BF)
        go(remote(pair_out.at[d], pair_in.at[d], pp_s.at[d], pp_r.at[d], at(z, q, other)))
        mine[...] = jnp.dot(active[qs:], down, preferred_element_type=F32)

    def finish(d):
        landing = pair_in.at[d]
        remote(landing, landing, pp_s.at[d], pp_r.at[d], at(z, q, other)).wait_recv()
        done = (mine[...] + pair_in[d].astype(F32)).astype(BF)
        back_out[d] = done.reshape(side, slots, width)
        back_in[d, q] = back_out[d, q]
        for k in range(1, side):
            qk = ahead(q, k, side)
            go(
                remote(
                    back_out.at[d, qk],
                    back_in.at[d, q],
                    rt_s.at[d, k],
                    rt_r.at[d, k],
                    at(z, qk, core),
                )
            )

    def combine(d):
        for k in range(1, side):
            qk = ahead(q, side - k, side)
            landing = back_in.at[d, qk]
            remote(
                landing, landing, rt_s.at[d, k], rt_r.at[d, k], at(z, qk, core)
            ).wait_recv()
        table = z_meta[d] if d else meta[z]
        weigh = jnp.transpose(table.astype(F32))[tokens : 3 * tokens].astype(BF)
        values = back_in[d].reshape(qs, width)
        both = jnp.dot(weigh, values, preferred_element_type=F32)
        part = both[:tokens] + both[tokens:]
        if d:
            part_out[d] = part.astype(BF)
            go(
                remote(
                    part_out.at[d],
                    part_in.at[d],
                    fn_s.at[d],
                    fn_r.at[d],
                    at(behind(d), q, core),
                )
            )
        else:
            total[...] = stream[...] + part

    pick(0)
    forward(0)
    compute(0)
    for d in range(1, planes):
        pick(d)
    for t in range(1, planes + 2):
        if t < planes:
            forward(t)
        if t - 1 < planes:
            finish(t - 1)
        if t < planes:
            compute(t)
        if 0 <= t - 2:
            combine(t - 2)
    result = total[...]
    for d in range(1, planes):
        landing = part_in.at[d]
        device = at(ahead(z, d, planes), q, core)
        remote(landing, landing, fn_s.at[d], fn_r.at[d], device).wait_recv()
        result = result + part_in[d].astype(F32)
    out[...] = result.astype(BF)
    for copy in sends:
        copy.wait_send()


def local(
    queries,
    cache,
    drafts,
    lengths,
    value_up,
    residual,
    norm_gain,
    w_gate,
    w_up,
    w_down,
    routes,
    combine_weights,
):
    tokens, width = residual.shape
    top = routes.shape[1]
    hidden = w_gate.shape[2]
    reqs, draft, heads, key = queries.shape
    queries = queries.reshape(reqs, draft * heads, key)
    cache = jnp.transpose(cache, (0, 2, 1))
    w_gate = jnp.transpose(w_gate, (0, 2, 1))
    w_up = jnp.transpose(w_up, (0, 2, 1))
    experts = lax.axis_size("ep") // 2
    capacity = min(tokens, 2 * (((tokens * top + experts - 1) // experts + 3) // 2))
    slots = up_to(capacity, 16)
    side = 4 if experts % 4 == 0 else 1
    planes = experts // side
    qs = side * slots
    lanes = up_to(3 * tokens + 1, 128)
    vm = pl.BlockSpec(memory_space=pltpu.VMEM)
    hbm = pl.BlockSpec(memory_space=pl.ANY)
    dma = pltpu.SemaphoreType.DMA
    block = (planes, side, slots, width)
    return pl.pallas_call(
        functools.partial(expert_kernel, planes, side, slots),
        out_shape=jax.ShapeDtypeStruct((tokens, width), BF),
        in_specs=[pl.BlockSpec(memory_space=pltpu.SMEM)] + [vm] * 5 + [hbm] * 6,
        out_specs=vm,
        scratch_shapes=[
            pltpu.VMEM(queries.shape, BF),
            pltpu.VMEM(cache.shape, BF),
            pltpu.VMEM(value_up.shape, BF),
            pltpu.VMEM((value_up.shape[1] // 128, tokens * heads, 128), F32),
            pltpu.VMEM((tokens, width), F32),
            pltpu.VMEM((tokens, width), BF),
            pltpu.VMEM((planes, qs, lanes), BF),
            pltpu.VMEM((hidden, width), BF),
            pltpu.VMEM((hidden, width), BF),
            pltpu.VMEM((hidden, width), BF),
            pltpu.VMEM((planes, tokens, width), BF),
            pltpu.VMEM((planes, qs, lanes), BF),
            pltpu.VMEM(block, BF),
            pltpu.VMEM((2,) + block, BF),
            pltpu.VMEM((qs, width), F32),
            pltpu.VMEM((planes, qs, width), BF),
            pltpu.VMEM((planes, qs, width), BF),
            pltpu.VMEM(block, BF),
            pltpu.VMEM(block, BF),
            pltpu.VMEM((planes, tokens, width), BF),
            pltpu.VMEM((planes, tokens, width), BF),
            pltpu.VMEM((tokens, width), F32),
            dma((reqs,)),
            dma((reqs,)),
            dma((1,)),
            dma((3,)),
        ]
        + [dma((planes,))] * 4
        + [dma((planes, side))] * 2
        + [dma((planes,))] * 4
        + [dma((planes, side))] * 2
        + [dma((planes,))] * 2,
        compiler_params=pltpu.CompilerParams(
            collective_id=0, has_side_effects=True, vmem_limit_bytes=60 * 2**20
        ),
    )(
        lengths,
        routes.T,
        combine_weights.T,
        drafts,
        residual,
        norm_gain[None],
        queries,
        cache,
        value_up,
        w_gate,
        w_up,
        w_down,
    )


def solution(mesh):
    placed = (
        P(("groups", "ep"), None, None, None),
        P(("groups", "ep"), None, None),
        P(("groups", "ep"), None, None),
        P(("groups", "ep")),
        P(),
        P(("groups", "ep"), None),
        P(),
        P("ep", None, None),
        P("ep", None, None),
        P("ep", None, None),
        P(("groups", "ep"), None),
        P(("groups", "ep"), None),
    )
    return jax.shard_map(
        local, mesh=mesh, in_specs=placed, out_specs=P(("groups", "ep"), None), check_vma=False
    )
```

profile of v0, /device:TPU:0, one launch (start us, length us, event | category | flops | bytes accessed | tf_op | source)
XLA Modules:
  0.0 56.2 jit_solution(17789351832460422520)
XLA Ops:
  0.0 54.6 %shard_map.118 = bf16[32,2048]{1,0:T(8,128)(2,1)} custom-call(s32[4]{0:T(128)} %lengths.1, s32[6,32]{1,0:T(8,128)} %bitcast.12, f32[6,32]{1,0:T(8,128)} %bitcast.13, bf16[4,8,576]{2,1,0:T(8,128)(2,1)} %drafts.1, bf16[32,2048]{1,0:T(8,128)(2,1)} %residual.1, f32[1,2048]{1,0:T(1,128)} %bitcast.11, bf16[4,128,576]{2,1,0:T(8,128)(2,1)} %bitcast.10, ...), custom_call_target="tpu_custom_call" | custom-call | tf_op jit(solution)/shard_map/pallas_call | solution.py:378
  54.6 1.6 %copy.14 = bf16[32,2048]{1,0:T(8,128)(2,1)} copy(bf16[32,2048]{1,0:T(8,128)(2,1)} %shard_map.118) | data formatting | bytes 262144
where the time goes:
time: 56.3 us; the launch traced here: 56.2 us
  Pallas kernels  54.6 us (97%)
  local copies, waits for them, and re-layouts  1.57 us (3%)
    pallas_call x1, Pallas kernels, local(): pl.pallas_call(functools.partial(expert_kernel, planes, side, slots), out...  54.6 us
    unnamed x1, local copies, waits for them, and re-layouts  1.57 us

commit v1 on v0

--- a/solution.py
+++ b/solution.py
@@ -68,6 +68,60 @@
         meta[e // side, at : at + slots] = block.astype(BF)
 
 
+def plan(planes):
+    if planes == 4:
+        order = [[0, 2, 1, 3], [1, 2, 0, 3], [2, 0, 1, 3], [3, 0, 2, 1]]
+        route = [
+            {0: [1], 1: [2], 2: [3]},
+            {1: [0, 2], 2: [3]},
+            {2: [3, 1], 1: [0]},
+            {3: [1, 2], 1: [0]},
+        ]
+        early = [[1, 1, 0, 1], [1, 0, 1, 1], [1, 1, 1, 1], [1, 1, 0, 1]]
+        steps = (
+            "P0 S R2b R3b",
+            "R2a P2 R1a R1b",
+            "F0 P1 F2 R3a",
+            "C2 P3 F1 C1",
+            "N2 F3 N1 C3",
+            "M2 N3 M1 C0",
+            "M3 N0 M0",
+        )
+        return order, route, early, sum([line.split() for line in steps], [])
+    order = [sorted(range(planes), key=lambda s: (abs(s - z), s)) for z in range(planes)]
+    route = []
+    for s in range(planes):
+        hops = {z: [z + 1] for z in range(s, planes - 1)}
+        hops.update({z: [z - 1] for z in range(1, s + 1)})
+        hops[s] = [z for z in (s + 1, s - 1) if 0 <= z < planes]
+        route.append(hops)
+    early = [[1] * planes for _ in range(planes)]
+    steps = ["P0", "S"]
+    for t in range(planes + 2):
+        for lag, kind in ((-1, "R"), (-1, "P"), (0, "F"), (0, "C"), (1, "N"), (2, "M")):
+            if 0 <= t - lag < planes:
+                steps.append(kind + str(t - lag) + "a" * (kind == "R"))
+    return order, route, early, steps
+
+
+def run_steps(script, pick, send_meta, relay, forward, compute, finish, combine):
+    table = {"P": pick, "F": forward, "C": compute, "N": finish, "M": combine}
+    for step in script:
+        if step == "S":
+            send_meta()
+        elif step[0] == "R":
+            relay(int(step[1]), int(step[2:] == "a"))
+        else:
+            table[step[0]](*[int(v) for v in step[1:]])
+
+
+def choose(values, index):
+    total = 0
+    for i, value in enumerate(values):
+        total = total + value * lax.div(1, 1 + (index - i) * (index - i))
+    return total
+
+
 def expert_kernel(
     planes,
     side,
@@ -90,7 +144,6 @@
     vup,
     mixes,
     stream,
-    normed,
     meta,
     w_gate,
     w_up,
@@ -126,7 +179,9 @@
     fn_s,
     fn_r,
 ):
-    tokens, width = normed.shape
+    tokens, width = stream.shape
+    pieces = zr_r.shape[1]
+    piece = tokens // pieces
     qs = side * slots
     me = lax.axis_index("ep")
     core = lax.rem(me, 2)
@@ -137,9 +192,6 @@
 
     def at(zz, qq, cc):
         return {"ep": (zz * side + qq) * 2 + cc}
-
-    def ahead(value, step, size):
-        return lax.rem(value + step, size)
 
     def remote(src, dst, send, recv, device):
         return pltpu.make_async_remote_copy(
@@ -150,6 +202,16 @@
             device_id=device,
             device_id_type=pl.DeviceIdType.MESH,
         )
+
+    near, route, early, script = plan(planes)
+    chunk = [z] + [choose([near[i][k] for i in range(planes)], z) for k in range(1, planes)]
+    flips = [
+        None,
+        q + 1 - 2 * lax.rem(q, 2),
+        lax.rem(q + 2, 4),
+        3 - q,
+    ]
+    turns = [3, 1, 2][: side - 1]
 
     reqs, draft_heads, _ = q_v.shape
     fetched = []
@@ -171,8 +233,8 @@
     for load in loads:
         load.start()
 
-    peers = [at(ahead(z, d, planes), q, core) for d in range(1, planes)]
-    peers += [at(z, ahead(q, d, side), core) for d in range(1, side)]
+    peers = [at(chunk[k], q, core) for k in range(1, planes)]
+    peers += [at(z, flips[j], core) for j in turns]
     peers += [at(z, q, other)]
     barrier = pltpu.get_barrier_semaphore()
     for peer in peers:
@@ -202,7 +264,7 @@
         )
     value = stream[...]
     level = lax.rsqrt(jnp.mean(value * value, axis=-1, keepdims=True) + 1e-06)
-    normed[...] = (value * level * gain[...]).astype(BF)
+    z_rows[z] = (value * level * gain[...]).astype(BF)
     pl.semaphore_wait(barrier, len(peers))
 
     sends = []
@@ -211,135 +273,189 @@
         copy.start()
         sends.append(copy)
 
-    for d in range(1, planes):
-        zd = ahead(z, d, planes)
-        device = at(zd, q, core)
-        go(remote(meta.at[zd], z_meta.at[d], zm_s.at[d], zm_r.at[d], device))
-        go(remote(normed, z_rows.at[d], zr_s.at[d], zr_r.at[d], device))
-
-    def behind(d):
-        return ahead(z, planes - d, planes)
-
-    def pick(d):
-        if d:
-            device = at(behind(d), q, core)
-            remote(z_meta.at[d], z_meta.at[d], zm_s.at[d], zm_r.at[d], device).wait_recv()
-            remote(normed, z_rows.at[d], zr_s.at[d], zr_r.at[d], device).wait_recv()
-            table, values = z_meta[d], z_rows[d]
+    def hop(k, p, way, target, valid):
+        s = chunk[k]
+        place = z_rows.at[s, p * piece : (p + 1) * piece]
+        copy = remote(place, place, zr_s.at[k, way, p], zr_r.at[s, p], at(target, q, core))
+        pl.when(valid)(copy.start)
+
+    def fans_of(k):
+        return [route[near[i][k]].get(i, []) for i in range(planes)]
+
+    def landed(k, p):
+        s = chunk[k]
+        place = z_rows.at[s, p * piece : (p + 1) * piece]
+        return remote(place, place, zr_s.at[k, 0, p], zr_r.at[s, p], at(s, q, core))
+
+    def onward(k):
+        fans = fans_of(k)
+        for p in range(pieces):
+            if k:
+                landed(k, p).wait_recv()
+            for way in range(max(len(fan) for fan in fans)):
+                valid = choose([int(way < len(fan)) for fan in fans], z)
+                target = choose([(fan + [0] * (way + 1))[way] for fan in fans], z)
+                hop(k, p, way, target, valid == 1)
+
+    def relay(k, when):
+        fans = fans_of(k)
+        now = [int(bool(fan) and early[i][k] == when) for i, fan in enumerate(fans)]
+        if any(now):
+            pl.when(choose(now, z) == 1)(lambda: onward(k))
+
+    def arrive(k):
+        leaf = choose([int(not fan) for fan in fans_of(k)], z)
+
+        @pl.when(leaf == 1)
+        def _():
+            for p in range(pieces):
+                landed(k, p).wait_recv()
+
+    onward(0)
+
+    def send_meta():
+        for k in range(1, planes):
+            zd = chunk[k]
+            go(remote(meta.at[zd], z_meta.at[z], zm_s.at[k], zm_r.at[z], at(zd, q, core)))
+
+    def pick(k):
+        s = chunk[k]
+        if k:
+            arrive(k)
+            device = at(s, q, core)
+            remote(z_meta.at[s], z_meta.at[s], zm_s.at[k], zm_r.at[s], device).wait_recv()
+            table, values = z_meta[s], z_rows[s]
         else:
-            table, values = meta[z], normed[...]
+            table, values = meta[z], z_rows[z]
         picked = jnp.dot(table[:, :tokens], values, preferred_element_type=F32).astype(BF)
-        stage[d] = picked.reshape(side, slots, width)
-        rows[core, d, q] = stage[d, q]
-        for k in range(1, side):
-            qk = ahead(q, k, side)
+        stage[k] = picked.reshape(side, slots, width)
+        for j in turns:
             go(
                 remote(
-                    stage.at[d, qk],
-                    rows.at[core, d, q],
-                    ip_s.at[d, k],
-                    ip_r.at[d, k],
-                    at(z, qk, core),
+                    stage.at[k, flips[j]],
+                    rows.at[core, s, q],
+                    ip_s.at[k, j],
+                    ip_r.at[s, j],
+                    at(z, flips[j], core),
                 )
             )
-
-    def forward(d):
-        for k in range(1, side):
-            qk = ahead(q, side - k, side)
-            landing = rows.at[core, d, qk]
+        rows[core, s, q] = stage[k, q]
+        cross(k, 0, q)
+
+    def cross(k, j, qk):
+        place = rows.at[core, chunk[k], qk]
+        go(remote(place, place, fw_s.at[k, j], fw_r.at[chunk[k], j], at(z, q, other)))
+
+    def forward(k):
+        s = chunk[k]
+        for j in turns[1:] + turns[:1]:
+            landing = rows.at[core, s, flips[j]]
             remote(
-                landing, landing, ip_s.at[d, k], ip_r.at[d, k], at(z, qk, core)
+                landing, landing, ip_s.at[k, j], ip_r.at[s, j], at(z, flips[j], core)
             ).wait_recv()
-        go(
-            remote(
-                rows.at[core, d], rows.at[core, d], fw_s.at[d], fw_r.at[d], at(z, q, other)
-            )
-        )
-
-    def compute(d):
-        landing = rows.at[other, d]
-        remote(landing, landing, fw_s.at[d], fw_r.at[d], at(z, q, other)).wait_recv()
-        if d == 0:
-            for load in loads:
-                load.wait()
-        x = jnp.concatenate(
-            [rows[other, d].reshape(qs, width), rows[core, d].reshape(qs, width)], axis=0
-        )
+            cross(k, j, flips[j])
+
+    def compute(*ks):
+        for k in ks:
+            s = chunk[k]
+            for j in [0] + turns:
+                landing = rows.at[other, s, flips[j] if j else q]
+                remote(
+                    landing, landing, fw_s.at[k, j], fw_r.at[s, j], at(z, q, other)
+                ).wait_recv()
+        while loads:
+            loads.pop(0).wait()
+        blocks = [rows[cc, chunk[k]].reshape(qs, width) for cc in (other, core) for k in ks]
+        x = jnp.concatenate(blocks, axis=0)
         gate = dot_rows(x, w_gate[...])
         upper = dot_rows(x, w_up[...])
         active = (gate / (1.0 + jnp.exp(-gate)) * upper).astype(BF)
-        down = w_down[...]
-        pair_out[d] = jnp.dot(active[:qs], down, preferred_element_type=F32).astype(BF)
-        go(remote(pair_out.at[d], pair_in.at[d], pp_s.at[d], pp_r.at[d], at(z, q, other)))
-        mine[...] = jnp.dot(active[qs:], down, preferred_element_type=F32)
-
-    def finish(d):
-        landing = pair_in.at[d]
-        remote(landing, landing, pp_s.at[d], pp_r.at[d], at(z, q, other)).wait_recv()
-        done = (mine[...] + pair_in[d].astype(F32)).astype(BF)
-        back_out[d] = done.reshape(side, slots, width)
-        back_in[d, q] = back_out[d, q]
-        for k in range(1, side):
-            qk = ahead(q, k, side)
+        half = width // 2
+        for p in range(2):
+            part = slice(p * half, (p + 1) * half)
+            both = jnp.dot(active, w_down[:, part], preferred_element_type=F32)
+            for i, k in enumerate(ks):
+                s = chunk[k]
+                pair_out[k, p] = both[i * qs : (i + 1) * qs].astype(BF)
+                go(
+                    remote(
+                        pair_out.at[k, p],
+                        pair_in.at[s, p],
+                        pp_s.at[k, p],
+                        pp_r.at[s, p],
+                        at(z, q, other),
+                    )
+                )
+                i += len(ks)
+                mine[k, p] = both[i * qs : (i + 1) * qs]
+
+    def finish(k):
+        s = chunk[k]
+        half = width // 2
+        for p in range(2):
+            landing = pair_in.at[s, p]
+            remote(
+                landing, landing, pp_s.at[k, p], pp_r.at[s, p], at(z, q, other)
+            ).wait_recv()
+            done = (mine[k, p] + pair_in[s, p].astype(F32)).astype(BF)
+            back_out[k, :, :, p * half : (p + 1) * half] = done.reshape(side, slots, half)
+        for j in turns:
             go(
                 remote(
-                    back_out.at[d, qk],
-                    back_in.at[d, q],
-                    rt_s.at[d, k],
-                    rt_r.at[d, k],
-                    at(z, qk, core),
+                    back_out.at[k, flips[j]],
+                    back_in.at[s, q],
+                    rt_s.at[k, j],
+                    rt_r.at[s, j],
+                    at(z, flips[j], core),
                 )
             )
-
-    def combine(d):
-        for k in range(1, side):
-            qk = ahead(q, side - k, side)
-            landing = back_in.at[d, qk]
+        back_in[s, q] = back_out[k, q]
+
+    def combine(k):
+        s = chunk[k]
+        for j in turns:
+            landing = back_in.at[s, flips[j]]
             remote(
-                landing, landing, rt_s.at[d, k], rt_r.at[d, k], at(z, qk, core)
+                landing, landing, rt_s.at[k, j], rt_r.at[s, j], at(z, flips[j], core)
             ).wait_recv()
-        table = z_meta[d] if d else meta[z]
+        table = z_meta[s] if k else meta[z]
         weigh = jnp.transpose(table.astype(F32))[tokens : 3 * tokens].astype(BF)
-        values = back_in[d].reshape(qs, width)
+        values = back_in[s].reshape(qs, width)
         both = jnp.dot(weigh, values, preferred_element_type=F32)
         part = both[:tokens] + both[tokens:]
-        if d:
-            part_out[d] = part.astype(BF)
+        if k:
+            part_out[k] = part.astype(BF)
             go(
                 remote(
-                    part_out.at[d],
-                    part_in.at[d],
-                    fn_s.at[d],
-                    fn_r.at[d],
-                    at(behind(d), q, core),
+                    part_out.at[k],
+                    part_in.at[z],
+                    fn_s.at[k],
+                    fn_r.at[z],
+                    at(s, q, core),
                 )
             )
         else:
             total[...] = stream[...] + part
 
-    pick(0)
-    forward(0)
-    compute(0)
-    for d in range(1, planes):
-        pick(d)
-    for t in range(1, planes + 2):
-        if t < planes:
-            forward(t)
-        if t - 1 < planes:
-            finish(t - 1)
-        if t < planes:
-            compute(t)
-        if 0 <= t - 2:
-            combine(t - 2)
+    run_steps(script, pick, send_meta, relay, forward, compute, finish, combine)
+
     result = total[...]
-    for d in range(1, planes):
-        landing = part_in.at[d]
-        device = at(ahead(z, d, planes), q, core)
-        remote(landing, landing, fn_s.at[d], fn_r.at[d], device).wait_recv()
-        result = result + part_in[d].astype(F32)
+    for k in range(1, planes):
+        s = chunk[k]
+        landing = part_in.at[s]
+        remote(landing, landing, fn_s.at[k], fn_r.at[s], at(s, q, core)).wait_recv()
+        result = result + part_in[s].astype(F32)
     out[...] = result.astype(BF)
     for copy in sends:
         copy.wait_send()
+    for k in range(planes):
+        fans = fans_of(k)
+        for p in range(pieces):
+            for way in range(max(len(fan) for fan in fans)):
+                valid = choose([int(way < len(fan)) for fan in fans], z)
+                place = z_rows.at[chunk[k], p * piece : (p + 1) * piece]
+                copy = remote(place, place, zr_s.at[k, way, p], zr_r.at[z, p], at(z, q, other))
+                pl.when(valid == 1)(copy.wait_send)
 
 
 def local(
@@ -386,7 +502,6 @@
             pltpu.VMEM(value_up.shape, BF),
             pltpu.VMEM((value_up.shape[1] // 128, tokens * heads, 128), F32),
             pltpu.VMEM((tokens, width), F32),
-            pltpu.VMEM((tokens, width), BF),
             pltpu.VMEM((planes, qs, lanes), BF),
             pltpu.VMEM((hidden, width), BF),
             pltpu.VMEM((hidden, width), BF),
@@ -395,9 +510,9 @@
             pltpu.VMEM((planes, qs, lanes), BF),
             pltpu.VMEM(block, BF),
             pltpu.VMEM((2,) + block, BF),
-            pltpu.VMEM((qs, width), F32),
-            pltpu.VMEM((planes, qs, width), BF),
-            pltpu.VMEM((planes, qs, width), BF),
+            pltpu.VMEM((planes, 2, qs, width // 2), F32),
+            pltpu.VMEM((planes, 2, qs, width // 2), BF),
+            pltpu.VMEM((planes, 2, qs, width // 2), BF),
             pltpu.VMEM(block, BF),
             pltpu.VMEM(block, BF),
             pltpu.VMEM((planes, tokens, width), BF),
@@ -408,9 +523,10 @@
             dma((1,)),
             dma((3,)),
         ]
-        + [dma((planes,))] * 4
-        + [dma((planes, side))] * 2
-        + [dma((planes,))] * 4
+        + [dma((planes, 3, 2)), dma((planes, 2))]
+        + [dma((planes,))] * 2
+        + [dma((planes, side))] * 4
+        + [dma((planes, 2))] * 2
         + [dma((planes, side))] * 2
         + [dma((planes,))] * 2,
         compiler_params=pltpu.CompilerParams(

time: 56.3 us -> 51 us (0.906)
  Pallas kernels: 54.6 us -> 49.3 us
    pallas_call x1, Pallas kernels: 54.6 us -> 49.3 us  [local(): pl.pallas_call(functools.partial(expert_kernel, planes, side, slots), out...]
where the time goes in v1:
time: 51 us; the launch traced here: 50.8 us
  Pallas kernels  49.3 us (97%)
  local copies, waits for them, and re-layouts  1.57 us (3%)
    pallas_call x1, Pallas kernels, local(): pl.pallas_call(functools.partial(expert_kernel, planes, side, slots), out...  49.3 us
    unnamed x1, local copies, waits for them, and re-layouts  1.57 us

profile of v1, /device:TPU:0, one launch (start us, length us, event | category | flops | bytes accessed | tf_op | source)
XLA Modules:
  0.0 50.8 jit_solution(4790091174428193788)
XLA Ops:
  0.0 49.3 %shard_map.118 = bf16[32,2048]{1,0:T(8,128)(2,1)} custom-call(s32[4]{0:T(128)} %lengths.1, s32[6,32]{1,0:T(8,128)} %bitcast.12, f32[6,32]{1,0:T(8,128)} %bitcast.13, bf16[4,8,576]{2,1,0:T(8,128)(2,1)} %drafts.1, bf16[32,2048]{1,0:T(8,128)(2,1)} %residual.1, f32[1,2048]{1,0:T(1,128)} %bitcast.11, bf16[4,128,576]{2,1,0:T(8,128)(2,1)} %bitcast.10, ...), custom_call_target="tpu_custom_call" | custom-call | tf_op jit(solution)/shard_map/pallas_call | solution.py:494
  49.3 1.6 %copy.14 = bf16[32,2048]{1,0:T(8,128)(2,1)} copy(bf16[32,2048]{1,0:T(8,128)(2,1)} %shard_map.118) | data formatting | bytes 262144

commit v2 on v1

--- a/solution.py
+++ b/solution.py
@@ -70,22 +70,22 @@
 
 def plan(planes):
     if planes == 4:
-        order = [[0, 2, 1, 3], [1, 2, 0, 3], [2, 0, 1, 3], [3, 0, 2, 1]]
+        order = [[0, 1, 3, 2], [1, 0, 2, 3], [2, 1, 3, 0], [3, 2, 1, 0]]
         route = [
             {0: [1], 1: [2], 2: [3]},
-            {1: [0, 2], 2: [3]},
+            {1: [2, 0], 2: [3]},
             {2: [3, 1], 1: [0]},
-            {3: [1, 2], 1: [0]},
+            {3: [2, 1], 1: [0]},
         ]
-        early = [[1, 1, 0, 1], [1, 0, 1, 1], [1, 1, 1, 1], [1, 1, 0, 1]]
+        early = [[1, 0, 0, 0], [1, 0, 1, 1], [1, 0, 0, 1], [1, 0, 0, 0]]
         steps = (
-            "P0 S R2b R3b",
-            "R2a P2 R1a R1b",
-            "F0 P1 F2 R3a",
-            "C2 P3 F1 C1",
-            "N2 F3 N1 C3",
-            "M2 N3 M1 C0",
-            "M3 N0 M0",
+            "P0 S R1b R1a",
+            "P1 R2a F0 R2b",
+            "R3a F1 R3b P3",
+            "C1 P2 F3 N1",
+            "C3 F2 N3 M1",
+            "C2 M3 N2 C0",
+            "N0 M2 M0",
         )
         return order, route, early, sum([line.split() for line in steps], [])
     order = [sorted(range(planes), key=lambda s: (abs(s - z), s)) for z in range(planes)]
@@ -127,11 +127,11 @@
     side,
     slots,
     lengths,
-    routes,
-    weights,
-    drafts,
-    residual,
-    gain,
+    routes_hbm,
+    weights_hbm,
+    drafts_hbm,
+    residual_hbm,
+    gain_hbm,
     q_hbm,
     cache_hbm,
     vup_hbm,
@@ -139,6 +139,11 @@
     up_hbm,
     down_hbm,
     out,
+    routes,
+    weights,
+    drafts,
+    residual,
+    gain,
     q_v,
     cache_v,
     vup,
@@ -160,6 +165,7 @@
     part_out,
     part_in,
     total,
+    s_sem,
     q_sem,
     c_sem,
     v_sem,
@@ -214,6 +220,20 @@
     turns = [3, 1, 2][: side - 1]
 
     reqs, draft_heads, _ = q_v.shape
+    small = [
+        pltpu.make_async_copy(src, dst, s_sem.at[i])
+        for i, (src, dst) in enumerate(
+            [
+                (routes_hbm, routes),
+                (weights_hbm, weights),
+                (drafts_hbm, drafts),
+                (residual_hbm, residual),
+                (gain_hbm, gain),
+            ]
+        )
+    ]
+    for load in small[:3]:
+        load.start()
     fetched = []
     for r in range(reqs):
         pair = [
@@ -223,6 +243,8 @@
         for load in pair:
             load.start()
         fetched.append(pair)
+    for load in small[3:]:
+        load.start()
     vup_load = pltpu.make_async_copy(vup_hbm, vup, v_sem.at[0])
     vup_load.start()
     loads = [
@@ -242,6 +264,8 @@
             barrier, inc=1, device_id=peer, device_id_type=pl.DeviceIdType.MESH
         )
 
+    for load in small[:3]:
+        load.wait()
     tables(routes, weights, meta, slots)
     heads, latent, head = vup.shape
     scale = (head + q_v.shape[2] - latent) ** (-0.5)
@@ -253,6 +277,8 @@
             mixes[g, r * draft_heads : (r + 1) * draft_heads] = mixed[
                 :, g * 128 : (g + 1) * 128
             ]
+    for load in small[3:]:
+        load.wait()
     vup_load.wait()
     for h in range(heads):
         value = jnp.concatenate(
@@ -493,10 +519,15 @@
     block = (planes, side, slots, width)
     return pl.pallas_call(
         functools.partial(expert_kernel, planes, side, slots),
-        out_shape=jax.ShapeDtypeStruct((tokens, width), BF),
-        in_specs=[pl.BlockSpec(memory_space=pltpu.SMEM)] + [vm] * 5 + [hbm] * 6,
+        out_shape=pltpu.VMEM((tokens, width), BF),
+        in_specs=[pl.BlockSpec(memory_space=pltpu.SMEM)] + [hbm] * 11,
         out_specs=vm,
         scratch_shapes=[
+            pltpu.VMEM((routes.shape[1], tokens), routes.dtype),
+            pltpu.VMEM((routes.shape[1], tokens), F32),
+            pltpu.VMEM(drafts.shape, BF),
+            pltpu.VMEM(residual.shape, BF),
+            pltpu.VMEM((1, width), F32),
             pltpu.VMEM(queries.shape, BF),
             pltpu.VMEM(cache.shape, BF),
             pltpu.VMEM(value_up.shape, BF),
@@ -518,6 +549,7 @@
             pltpu.VMEM((planes, tokens, width), BF),
             pltpu.VMEM((planes, tokens, width), BF),
             pltpu.VMEM((tokens, width), F32),
+            dma((5,)),
             dma((reqs,)),
             dma((reqs,)),
             dma((1,)),

time: 51 us -> 47.4 us (0.929)
  the two profiles are of different devices: /device:TPU:0 before, /device:TPU:25 now
where the time goes in v2:
time: 47.4 us; the launch traced here: 47.3 us
  Pallas kernels  46.6 us (98%)
  local copies, waits for them, and re-layouts  0.66 us (1%)
    pallas_call x1, Pallas kernels, local(): pl.pallas_call(functools.partial(expert_kernel, planes, side, slots), out...  46.6 us

profile of v2, /device:TPU:25, one launch (start us, length us, event | category | flops | bytes accessed | tf_op | source)
XLA Modules:
  0.0 47.3 jit_solution(13605024044266864534)
XLA Ops:
  0.0 46.6 %shard_map.118 = bf16[32,2048]{1,0:T(8,128)(2,1)S(1)} custom-call(s32[4]{0:T(128)} %lengths.1, s32[6,32]{1,0:T(8,128)} %bitcast.12, f32[6,32]{1,0:T(8,128)} %bitcast.13, bf16[4,8,576]{2,1,0:T(8,128)(2,1)} %drafts_hbm.1, bf16[32,2048]{1,0:T(8,128)(2,1)} %residual_hbm.1, f32[1,2048]{1,0:T(1,128)} %bitcast.11, bf16[4,128,576]{2,1,0:T(8,128)(2,1)} %bitcast.10, ...), custom_call_target="tpu_custom_call" | custom-call | tf_op jit(solution)/shard_map/pallas_call | solution.py:520
  46.6 0.7 %copy.14 = bf16[32,2048]{1,0:T(8,128)(2,1)} copy(bf16[32,2048]{1,0:T(8,128)(2,1)S(1)} %shard_map.118) | data formatting | bytes 262144

commit v3 on v2

--- a/solution.py
+++ b/solution.py
@@ -77,15 +77,15 @@
             {2: [3, 1], 1: [0]},
             {3: [2, 1], 1: [0]},
         ]
-        early = [[1, 0, 0, 0], [1, 0, 1, 1], [1, 0, 0, 1], [1, 0, 0, 0]]
+        early = [[1, 0, 0, 0], [1, 0, 1, 0], [1, 0, 0, 1], [1, 0, 0, 0]]
         steps = (
             "P0 S R1b R1a",
-            "P1 R2a F0 R2b",
+            "P1 F0 R2b R2a",
             "R3a F1 R3b P3",
             "C1 P2 F3 N1",
             "C3 F2 N3 M1",
-            "C2 M3 N2 C0",
-            "N0 M2 M0",
+            "C20 M3 N2 N0",
+            "M2 M0",
         )
         return order, route, early, sum([line.split() for line in steps], [])
     order = [sorted(range(planes), key=lambda s: (abs(s - z), s)) for z in range(planes)]
@@ -126,7 +126,7 @@
     planes,
     side,
     slots,
-    lengths,
+    lengths_hbm,
     routes_hbm,
     weights_hbm,
     drafts_hbm,
@@ -139,6 +139,7 @@
     up_hbm,
     down_hbm,
     out,
+    lengths,
     routes,
     weights,
     drafts,
@@ -165,6 +166,7 @@
     part_out,
     part_in,
     total,
+    far_sem,
     s_sem,
     q_sem,
     c_sem,
@@ -229,10 +231,11 @@
                 (drafts_hbm, drafts),
                 (residual_hbm, residual),
                 (gain_hbm, gain),
+                (lengths_hbm, lengths),
             ]
         )
     ]
-    for load in small[:3]:
+    for load in small[2:3] + small[5:]:
         load.start()
     fetched = []
     for r in range(reqs):
@@ -243,7 +246,7 @@
         for load in pair:
             load.start()
         fetched.append(pair)
-    for load in small[3:]:
+    for load in small[:2] + small[3:5]:
         load.start()
     vup_load = pltpu.make_async_copy(vup_hbm, vup, v_sem.at[0])
     vup_load.start()
@@ -255,30 +258,45 @@
     for load in loads:
         load.start()
 
-    peers = [at(chunk[k], q, core) for k in range(1, planes)]
-    peers += [at(z, flips[j], core) for j in turns]
-    peers += [at(z, q, other)]
+    def flag(test, k):
+        return choose([int(test(i, near[i][k])) for i in range(planes)], z) == 1
+
+    def signal(semaphore, device):
+        pl.semaphore_signal(
+            semaphore, inc=1, device_id=device, device_id_type=pl.DeviceIdType.MESH
+        )
+
     barrier = pltpu.get_barrier_semaphore()
-    for peer in peers:
-        pl.semaphore_signal(
-            barrier, inc=1, device_id=peer, device_id_type=pl.DeviceIdType.MESH
+    for j in turns:
+        signal(barrier, at(z, flips[j], core))
+    signal(barrier, at(z, q, other))
+    for k in range(1, planes):
+        pl.when(flag(lambda i, d: d >= i - 1, k))(
+            functools.partial(signal, barrier, at(chunk[k], q, core))
         )
-
-    for load in small[:3]:
+    heard = [sum(s != i and s <= i + 1 for s in range(planes)) for i in range(planes)]
+
+    for load in small[2:3] + small[5:]:
         load.wait()
-    tables(routes, weights, meta, slots)
     heads, latent, head = vup.shape
     scale = (head + q_v.shape[2] - latent) ** (-0.5)
     for r in range(reqs):
+        if r == reqs - 1:
+            pl.semaphore_wait(barrier, len(turns) + 1 + choose(heard, z))
+            for k in range(1, planes):
+                pl.when(flag(lambda i, d: d < i - 1, k))(
+                    functools.partial(signal, far_sem.at[z], at(chunk[k], q, core))
+                )
         for load in fetched[r]:
             load.wait()
-        mixed = attend(q_v[r], cache_v[r], drafts[r], lengths[r], heads, latent, scale)
+        mixed = attend(q_v[r], cache_v[r], drafts[r], lengths[:, r : r + 1], heads, latent, scale)
         for g in range(latent // 128):
             mixes[g, r * draft_heads : (r + 1) * draft_heads] = mixed[
                 :, g * 128 : (g + 1) * 128
             ]
-    for load in small[3:]:
+    for load in small[:2] + small[3:5]:
         load.wait()
+    tables(routes, weights, meta, slots)
     vup_load.wait()
     for h in range(heads):
         value = jnp.concatenate(
@@ -291,8 +309,6 @@
     value = stream[...]
     level = lax.rsqrt(jnp.mean(value * value, axis=-1, keepdims=True) + 1e-06)
     z_rows[z] = (value * level * gain[...]).astype(BF)
-    pl.semaphore_wait(barrier, len(peers))
-
     sends = []
 
     def go(copy):
@@ -342,6 +358,9 @@
     def send_meta():
         for k in range(1, planes):
             zd = chunk[k]
+            pl.when(flag(lambda i, d: d > i + 1, k))(
+                functools.partial(pl.semaphore_wait, far_sem.at[zd], 1)
+            )
             go(remote(meta.at[zd], z_meta.at[z], zm_s.at[k], zm_r.at[z], at(zd, q, core)))
 
     def pick(k):
@@ -520,9 +539,10 @@
     return pl.pallas_call(
         functools.partial(expert_kernel, planes, side, slots),
         out_shape=pltpu.VMEM((tokens, width), BF),
-        in_specs=[pl.BlockSpec(memory_space=pltpu.SMEM)] + [hbm] * 11,
+        in_specs=[hbm] * 12,
         out_specs=vm,
         scratch_shapes=[
+            pltpu.VMEM((1, reqs), lengths.dtype),
             pltpu.VMEM((routes.shape[1], tokens), routes.dtype),
             pltpu.VMEM((routes.shape[1], tokens), F32),
             pltpu.VMEM(drafts.shape, BF),
@@ -549,13 +569,14 @@
             pltpu.VMEM((planes, tokens, width), BF),
             pltpu.VMEM((planes, tokens, width), BF),
             pltpu.VMEM((tokens, width), F32),
-            dma((5,)),
+            pltpu.SemaphoreType.REGULAR((planes,)),
+            dma((6,)),
             dma((reqs,)),
             dma((reqs,)),
             dma((1,)),
             dma((3,)),
         ]
-        + [dma((planes, 3, 2)), dma((planes, 2))]
+        + [dma((planes, 3, 1)), dma((planes, 1))]
         + [dma((planes,))] * 2
         + [dma((planes, side))] * 4
         + [dma((planes, 2))] * 2
@@ -565,7 +586,7 @@
             collective_id=0, has_side_effects=True, vmem_limit_bytes=60 * 2**20
         ),
     )(
-        lengths,
+        lengths[None],
         routes.T,
         combine_weights.T,
         drafts,

time: 47.4 us -> 46.4 us (0.979)
  the two profiles are of different devices: /device:TPU:25 before, /device:TPU:8 now
where the time goes in v3:
time: 46.4 us; the launch traced here: 46.3 us
  Pallas kernels  45.6 us (98%)
  local copies, waits for them, and re-layouts  0.66 us (1%)
    pallas_call x1, Pallas kernels, local(): pl.pallas_call(functools.partial(expert_kernel, planes, side, slots), out...  45.6 us

profile of v3, /device:TPU:8, one launch (start us, length us, event | category | flops | bytes accessed | tf_op | source)
XLA Modules:
  0.0 46.3 jit_solution(12070406996682581806)
XLA Ops:
  0.0 45.6 %shard_map.118 = bf16[32,2048]{1,0:T(8,128)(2,1)S(1)} custom-call(s32[1,4]{1,0:T(1,128)} %bitcast.15, s32[6,32]{1,0:T(8,128)} %bitcast.13, f32[6,32]{1,0:T(8,128)} %bitcast.14, bf16[4,8,576]{2,1,0:T(8,128)(2,1)} %drafts_hbm.1, bf16[32,2048]{1,0:T(8,128)(2,1)} %residual_hbm.1, f32[1,2048]{1,0:T(1,128)} %bitcast.12, bf16[4,128,576]{2,1,0:T(8,128)(2,1)} %bitcast.11, ...), custom_call_target="tpu_custom_call" | custom-call | tf_op jit(solution)/shard_map/pallas_call | solution.py:539
  45.6 0.7 %copy.14 = bf16[32,2048]{1,0:T(8,128)(2,1)} copy(bf16[32,2048]{1,0:T(8,128)(2,1)S(1)} %shard_map.118) | data formatting | bytes 262144

commit v4 on v3

--- a/solution.py
+++ b/solution.py
@@ -310,6 +310,7 @@
     level = lax.rsqrt(jnp.mean(value * value, axis=-1, keepdims=True) + 1e-06)
     z_rows[z] = (value * level * gain[...]).astype(BF)
     sends = []
+    returns = []
 
     def go(copy):
         copy.start()
@@ -470,27 +471,16 @@
         part = both[:tokens] + both[tokens:]
         if k:
             part_out[k] = part.astype(BF)
-            go(
-                remote(
-                    part_out.at[k],
-                    part_in.at[z],
-                    fn_s.at[k],
-                    fn_r.at[z],
-                    at(s, q, core),
-                )
+            copy = remote(
+                part_out.at[k], part_in.at[z], fn_s.at[k], fn_r.at[z], at(s, q, core)
             )
+            copy.start()
+            returns.append(copy)
         else:
             total[...] = stream[...] + part
 
     run_steps(script, pick, send_meta, relay, forward, compute, finish, combine)
 
-    result = total[...]
-    for k in range(1, planes):
-        s = chunk[k]
-        landing = part_in.at[s]
-        remote(landing, landing, fn_s.at[k], fn_r.at[s], at(s, q, core)).wait_recv()
-        result = result + part_in[s].astype(F32)
-    out[...] = result.astype(BF)
     for copy in sends:
         copy.wait_send()
     for k in range(planes):
@@ -501,6 +491,15 @@
                 place = z_rows.at[chunk[k], p * piece : (p + 1) * piece]
                 copy = remote(place, place, zr_s.at[k, way, p], zr_r.at[z, p], at(z, q, other))
                 pl.when(valid == 1)(copy.wait_send)
+    result = total[...]
+    for k in range(1, planes):
+        s = chunk[k]
+        landing = part_in.at[s]
+        remote(landing, landing, fn_s.at[k], fn_r.at[s], at(s, q, core)).wait_recv()
+        result = result + part_in[s].astype(F32)
+    out[...] = result.astype(BF)
+    for copy in returns:
+        copy.wait_send()
 
 
 def local(

time: 46.4 us -> 46.4 us (level)
  no operation moved by 1% of the time
where the time goes in v4:
time: 46.4 us; the launch traced here: 46.2 us
  Pallas kernels  45.6 us (98%)
  local copies, waits for them, and re-layouts  0.66 us (1%)
    pallas_call x1, Pallas kernels, local(): pl.pallas_call(functools.partial(expert_kernel, planes, side, slots), out...  45.6 us

profile of v4, /device:TPU:8, one launch (start us, length us, event | category | flops | bytes accessed | tf_op | source)
XLA Modules:
  0.0 46.2 jit_solution(4758019399323305385)
XLA Ops:
  0.0 45.6 %shard_map.118 = bf16[32,2048]{1,0:T(8,128)(2,1)S(1)} custom-call(s32[1,4]{1,0:T(1,128)} %bitcast.15, s32[6,32]{1,0:T(8,128)} %bitcast.13, f32[6,32]{1,0:T(8,128)} %bitcast.14, bf16[4,8,576]{2,1,0:T(8,128)(2,1)} %drafts_hbm.1, bf16[32,2048]{1,0:T(8,128)(2,1)} %residual_hbm.1, f32[1,2048]{1,0:T(1,128)} %bitcast.12, bf16[4,128,576]{2,1,0:T(8,128)(2,1)} %bitcast.11, ...), custom_call_target="tpu_custom_call" | custom-call | tf_op jit(solution)/shard_map/pallas_call | solution.py:538
  45.6 0.7 %copy.14 = bf16[32,2048]{1,0:T(8,128)(2,1)} copy(bf16[32,2048]{1,0:T(8,128)(2,1)S(1)} %shard_map.118) | data formatting | bytes 262144
